TPU v7x, 128 devices: a whole 4x4x4 slice. The times are simulated.
128 devices in a mesh: section: 2 (over y_hi), expert: 8 (over z, core), hid: 8 (over x, y_lo).
Axes of the slice: x: 4, y: 4 (y_hi: 2, y_lo: 2; y = y_hi * 2 + y_lo), z: 4, core: 2. Of those that a mesh axis runs over, the one named last changes fastest.
Arguments:
- saved_input: bfloat16 [2, 1024, 4096], P('section', 'expert', 'hid'), may hold values from -6 to 6
- cotangent: bfloat16 [2, 1024, 4096], P('section', 'expert', 'hid'), may hold values from -6 to 6
- next_input: bfloat16 [2, 1024, 4096], P('section', 'expert', 'hid'), may hold values from -6 to 6
- routes_saved: int32 [2, 1024, 2], P('section', 'expert'), may hold values from 0 to 7, all different within a row; in each aligned block of 128 rows (0 to 127, 128 to 255, ..., all dimensions but the last counted through in order) at most 48 rows name the same one
- routes_next: int32 [2, 1024, 2], P('section', 'expert'), may hold values from 0 to 7, all different within a row; in each aligned block of 128 rows (0 to 127, 128 to 255, ..., all dimensions but the last counted through in order) at most 48 rows name the same one
- norm_gain: float32 [2, 4096], P('section', 'hid'), may hold values from 0.1 to 1.9
- router: float32 [2, 4096, 8], P('section', 'hid'), may hold values from -0.18 to 0.18
- expert_gate: bfloat16 [2, 8, 4096, 7168], P('section', 'expert', None, 'hid'), may hold values from -0.09375 to 0.09375
- expert_up: bfloat16 [2, 8, 4096, 7168], P('section', 'expert', None, 'hid'), may hold values from -0.09375 to 0.09375
- expert_down: bfloat16 [2, 8, 7168, 4096], P('section', 'expert', 'hid'), may hold values from -0.0625 to 0.0625
Outputs:
- leaving: bfloat16 [2, 1024, 4096], P('section', 'expert', 'hid')
- arriving: bfloat16 [2, 1024, 4096], P('section', 'expert', 'hid')
Inputs may be any that keep to these rules, and one draw needn't show every extreme that they name: `routes_saved`: A token's two ids differ. In each aligned block of 128 tokens of a section no expert is named by more than 48 tokens, and some block names some expert exactly 48 times. `routes_next`: A token's two ids differ. In each aligned block of 128 tokens of a section no expert is named by more than 48 tokens, and some block names some expert exactly 48 times.
All inputs are finite; a program needn't handle non-finite values.
Results may differ from a plain program's by a relative error of at most 0.0052.
Values may be sent and summed in bfloat16 or wider, within the bound.
No kernel may reach another device: no remote copies, remote signals or barrier semaphores. Data moves between devices by JAX's collectives and lax.ppermute only.
A program may use at most 128 MiB of HBM per device.

v0:
```python
import jax
import jax.numpy as jnp
from jax import lax
from jax.sharding import PartitionSpec as P

EPSILON = 1e-05
HIGHEST = lax.Precision.HIGHEST
CONTRACT = (((1,), (1,)), ((), ()))


def partner(block, axis, bit):
    count = lax.axis_size(axis)
    route = []
    for low in range(count):
        high = low | 1 << bit
        if high != low and high < count:
            route += [(low, high), (high, low)]
    return lax.ppermute(block, axis, route)


def norm_terms(values, gain, table):
    squares = jnp.sum(values * values, axis=1)
    partial_value = jnp.dot(values * gain[None, :], table, precision=HIGHEST)
    return (squares, partial_value)


def finish_norm(values, squares, partial_value, gain, width):
    scale = lax.rsqrt(squares / width + EPSILON)
    normed = (values * scale[:, None] * gain[None, :]).astype(jnp.bfloat16)
    return (scale, normed, scale[:, None] * partial_value)


def placing(routes, logits, capacity):
    experts = logits.shape[1]
    tokens = routes.shape[0]
    labels = jnp.arange(experts, dtype=jnp.int32)
    flat_ids = routes.reshape(-1)
    onehot = (flat_ids[:, None] == labels[None, :]).astype(jnp.int32)
    ranked = jnp.cumsum(onehot, axis=0) - onehot
    places = jnp.sum(ranked * onehot, axis=1)
    targets = (flat_ids * capacity + places).reshape(tokens, 2)
    first_hit = (routes[:, 0:1] == labels[None, :]).astype(jnp.float32)
    second_hit = (routes[:, 1:2] == labels[None, :]).astype(jnp.float32)
    first_logit = jnp.sum(logits * first_hit, axis=1)
    second_logit = jnp.sum(logits * second_hit, axis=1)
    first_prob = jax.nn.sigmoid(first_logit - second_logit)
    second_prob = jax.nn.sigmoid(second_logit - first_logit)
    all_slots = jnp.arange(experts * capacity, dtype=jnp.int32)
    slot_map = jnp.any(targets[None, :, :] == all_slots[:, None, None], axis=2).astype(jnp.bfloat16)
    return (targets, first_prob, second_prob, first_hit - second_hit, slot_map)


def row_buffer(slot_map, rows):
    return jnp.dot(slot_map, rows, preferred_element_type=jnp.float32).astype(jnp.bfloat16)


def blend(rows, targets, first_prob, second_prob):
    return first_prob[:, None] * rows[targets[:, 0]] + second_prob[:, None] * rows[targets[:, 1]]


def add_products(matrices, pieces):
    gate_matrix, up_matrix, down_matrix = matrices
    saved_rows, cot_rows, next_rows = pieces
    gate_saved = jnp.dot(saved_rows, gate_matrix, preferred_element_type=jnp.float32)
    up_saved = jnp.dot(saved_rows, up_matrix, preferred_element_type=jnp.float32)
    grad_hidden = lax.dot_general(
        cot_rows, down_matrix, CONTRACT, preferred_element_type=jnp.float32
    )
    gate_next = jnp.dot(next_rows, gate_matrix, preferred_element_type=jnp.float32)
    up_next = jnp.dot(next_rows, up_matrix, preferred_element_type=jnp.float32)
    return (gate_saved, up_saved, grad_hidden, gate_next, up_next)


def per_device(
    saved_input,
    cotangent,
    next_input,
    routes_saved,
    routes_next,
    norm_gain,
    router,
    expert_gate,
    expert_up,
    expert_down,
):
    gain = norm_gain[0]
    table = router[0]
    gate_matrix = expert_gate[0, 0]
    up_matrix = expert_up[0, 0]
    down_matrix = expert_down[0, 0]
    matrices = (gate_matrix, up_matrix, down_matrix)
    width = gate_matrix.shape[0]
    cot_rows = cotangent[0]
    values_saved = saved_input[0].astype(jnp.float32)
    values_next = next_input[0].astype(jnp.float32)
    squares_saved, partial_saved = norm_terms(values_saved, gain, table)
    squares_next, partial_next = norm_terms(values_next, gain, table)
    squares_saved, partial_saved, squares_next, partial_next = lax.psum(
        (squares_saved, partial_saved, squares_next, partial_next), "hid"
    )
    scale_saved, normed_saved, logits_saved = finish_norm(
        values_saved, squares_saved, partial_saved, gain, width
    )
    scale_next, normed_next, logits_next = finish_norm(
        values_next, squares_next, partial_next, gain, width
    )
    tokens = values_saved.shape[0]
    experts = lax.axis_size("expert")
    capacity = 3 * tokens // experts
    targets_saved, first_saved, second_saved, diff_saved, map_saved = placing(
        routes_saved[0], logits_saved, capacity
    )
    targets_next, first_next, second_next, diff_next, map_next = placing(
        routes_next[0], logits_next, capacity
    )
    packed = (
        row_buffer(map_saved, normed_saved),
        row_buffer(map_saved, cot_rows),
        row_buffer(map_next, normed_next),
    )
    moved = (
        lax.all_to_all(packed[0], "expert", split_axis=0, concat_axis=0, tiled=True),
        lax.all_to_all(packed[1], "expert", split_axis=0, concat_axis=0, tiled=True),
        lax.all_to_all(packed[2], "expert", split_axis=0, concat_axis=0, tiled=True),
    )
    sums = add_products(
        matrices,
        (
            lax.all_gather(moved[0], "hid", axis=1, tiled=True),
            lax.all_gather(moved[1], "hid", axis=1, tiled=True),
            lax.all_gather(moved[2], "hid", axis=1, tiled=True),
        ),
    )
    gate_saved, up_saved, grad_hidden, gate_next, up_next = sums
    sig_saved = jax.nn.sigmoid(gate_saved)
    silu_saved = gate_saved * sig_saved
    hidden_saved = (silu_saved * up_saved).astype(jnp.bfloat16)
    dot_terms = jnp.sum(grad_hidden * hidden_saved.astype(jnp.float32), axis=1)
    row_dots = lax.psum(dot_terms, "hid")
    grad_gate = (
        grad_hidden * up_saved * (sig_saved * (1.0 + gate_saved * (1.0 - sig_saved)))
    ).astype(jnp.bfloat16)
    grad_up = (grad_hidden * silu_saved).astype(jnp.bfloat16)
    back_part = lax.dot_general(
        grad_gate, gate_matrix, CONTRACT, preferred_element_type=jnp.float32
    ) + lax.dot_general(grad_up, up_matrix, CONTRACT, preferred_element_type=jnp.float32)
    silu_next = gate_next * jax.nn.sigmoid(gate_next)
    hidden_next = (silu_next * up_next).astype(jnp.bfloat16)
    out_part = jnp.dot(hidden_next, down_matrix, preferred_element_type=jnp.float32)
    back_sum, out_sum = (
        lax.psum_scatter(back_part, "hid", scatter_dimension=1, tiled=True),
        lax.psum_scatter(out_part, "hid", scatter_dimension=1, tiled=True),
    )
    back_home, dots_home, out_home = (
        lax.all_to_all(back_sum, "expert", split_axis=0, concat_axis=0, tiled=True),
        lax.all_to_all(row_dots, "expert", split_axis=0, concat_axis=0, tiled=True),
        lax.all_to_all(out_sum, "expert", split_axis=0, concat_axis=0, tiled=True),
    )
    mixed_saved = blend(back_home, targets_saved, first_saved, second_saved)
    branch_next = blend(out_home, targets_next, first_next, second_next)
    forward_out = (values_next + branch_next).astype(jnp.bfloat16)
    grad_logit = (
        (dots_home[targets_saved[:, 0]] - dots_home[targets_saved[:, 1]])
        * first_saved
        * second_saved
    )
    grad_normed = mixed_saved + jnp.dot(
        grad_logit[:, None] * diff_saved, table.T, precision=HIGHEST
    )
    scaled_grad = grad_normed * gain[None, :]
    inner = lax.psum(jnp.sum(scaled_grad * values_saved, axis=1), "hid")
    cube = scale_saved * scale_saved * scale_saved
    grad_input = (
        cot_rows.astype(jnp.float32)
        + scale_saved[:, None] * scaled_grad
        - values_saved * cube[:, None] * (inner / width)[:, None]
    )
    grad_input = grad_input.astype(jnp.bfloat16)
    first_section = lax.axis_index("section") == 0
    outgoing = jnp.where(first_section, forward_out, grad_input)
    leaving = jnp.where(first_section, grad_input, forward_out)
    arriving = partner(outgoing, "section", 0)
    return (leaving[None], arriving[None])


def solution(mesh):
    placed = (
        P("section", "expert", "hid"),
        P("section", "expert", "hid"),
        P("section", "expert", "hid"),
        P("section", "expert", None),
        P("section", "expert", None),
        P("section", "hid"),
        P("section", "hid", None),
        P("section", "expert", None, "hid"),
        P("section", "expert", None, "hid"),
        P("section", "expert", "hid", None),
    )
    return jax.shard_map(
        per_device,
        mesh=mesh,
        in_specs=placed,
        out_specs=(P("section", "expert", "hid"), P("section", "expert", "hid")),
        check_vma=False,
    )
```

profile of v0, /device:TPU:0, one launch (start us, length us, event | category | flops | bytes accessed | tf_op | source)
XLA Modules:
  0.0 648.1 jit_solution(6616434694353465557)
XLA Ops:
  9.4 19.8 %psum.42 = f32[128]{0:T(128)S(1)} all-reduce(f32[128]{0:T(128)S(1)} %fusion.39), channel_id=1, replica_groups=mesh['section'=2,'expert'=8,'hid'=8] {'hid'}, use_global_device_ids=true, to_apply=%region_1.0 | all-reduce | flops 128 | bytes 1024 | tf_op jit(solution)/shard_map/psum | solution.py:98
  32.3 14.2 %all_to_all.72 = bf16[8,48,512]{2,1,0:T(8,128)(2,1)} all-to-all(bf16[8,48,512]{2,1,0:T(8,128)(2,1)S(1)} %bitcast.152), channel_id=1, replica_groups=mesh['section'=2,'expert'=8,'hid'=8] {'expert'}, dimensions={0} | all-to-all | bytes 786432 | tf_op jit(solution)/shard_map/all_to_all | solution.py:122
  46.8 12.0 %all_to_all.73 = bf16[8,48,512]{2,1,0:T(8,128)(2,1)} all-to-all(bf16[8,48,512]{2,1,0:T(8,128)(2,1)S(1)} %bitcast.150), channel_id=1, replica_groups=mesh['section'=2,'expert'=8,'hid'=8] {'expert'}, dimensions={0} | all-to-all | bytes 786432 | tf_op jit(solution)/shard_map/all_to_all | solution.py:123
  58.9 54.5 %all-gather.6.cloned.1.call-done = bf16[384,4096]{1,0:T(8,128)(2,1)} async-done(((bf16[384,512]{1,0:T(8,128)(2,1)}), bf16[384,4096]{1,0:T(8,128)(2,1)}) %all-gather.6.cloned.1.call-update) | async-done | bytes 3145744 | tf_op jit(solution)/shard_map/all_gather | solution.py:129
  113.5 9.0 %fusion.4 = f32[384,896]{1,0:T(8,128)S(1)} fusion(bf16[384,4096]{1,0:T(8,128)(2,1)} %all-gather.6.cloned.1.call-done, bf16[1,1,4096,896]{3,2,1,0:T(8,128)(2,1)} %param.17), kind=kOutput, calls=%fused_computation.10 | convolution fusion | flops 2818572288 | bytes 11862016 | tf_op jit(solution)/shard_map/dot_general | solution.py:64
  122.5 5.7 fusion.10
  128.2 58.1 %all-gather.4.cloned.1.call-done = bf16[384,4096]{1,0:T(8,128)(2,1)} async-done(((bf16[384,512]{1,0:T(8,128)(2,1)}), bf16[384,4096]{1,0:T(8,128)(2,1)}) %all-gather.4.cloned.1.call-update) | async-done | bytes 3145744 | tf_op jit(solution)/shard_map/all_gather | solution.py:130
  186.3 8.5 %multiply_reduce_fusion = (f32[384]{0:T(512)S(1)}, f32[384,896]{1,0:T(8,128)S(1)}) fusion(f32[384,896]{1,0:T(8,128)S(1)} %fusion.10, f32[384,896]{1,0:T(8,128)S(1)} %fusion.4, bf16[384,4096]{1,0:T(8,128)(2,1)} %all-gather.4.cloned.1.call-done, bf16[1,1,896,4096]{3,2,1,0:T(8,128)(2,1)} %param.19), kind=kOutput, calls=%fused_computation.24 | convolution fusion | flops 2821668352 | bytes 14616064 | tf_op jit(solution)/shard_map/dot_general | solution.py:66
  194.8 6.1 fusion.2
  200.9 10.1 %fusion.16 = f32[384,4096]{1,0:T(8,128)} fusion(f32[384,4096]{1,0:T(8,128)S(1)} %fusion.2, bf16[1,1,4096,896]{3,2,1,0:T(8,128)(2,1)} %param.18, f32[384,896]{1,0:T(8,128)S(1)} %get-tuple-element.30, f32[384,896]{1,0:T(8,128)S(1)} %fusion.4), kind=kOutput, calls=%fused_computation.22 | convolution fusion | flops 2822209536 | bytes 22675456 | tf_op jit(solution)/shard_map/dot_general | solution.py:146
  214.0 26.3 %all-reduce.1 = (f32[128,8]{0,1:T(8,128)S(1)}, f32[8,48,1]{1,0,2:T(8,128)}) all-reduce(f32[128,8]{0,1:T(8,128)S(1)} %fusion.47, f32[8,48,1]{1,0,2:T(8,128)S(1)} %all_to_all.57), channel_id=1, replica_groups=mesh['section'=2,'expert'=8,'hid'=8] {'hid'}, use_global_device_ids=true, to_apply=%region_2.0 | all-reduce | flops 1408 | bytes 11264 | tf_op jit(solution)/shard_map/psum | solution.py:98
  240.3 4.5 all-to-all-start.3
  245.0 5.0 all-to-all-done.3
  250.0 92.7 %reduce-scatter.3.cloned.1.call-done = f32[384,512]{1,0:T(8,128)} async-done(((f32[384,4096]{1,0:T(8,128)}), f32[384,512]{1,0:T(8,128)}) %reduce-scatter.3.cloned.1.call-update) | async-done | bytes 786448 | tf_op jit(solution)/shard_map/reduce_scatter | solution.py:151
  342.7 4.4 all-to-all-start.2
  351.5 8.8 %all-to-all-done.2 = f32[8,48,512]{2,1,0:T(8,128)S(1)} async-done(((f32[8,48,512]{2,1,0:T(8,128)}), f32[8,48,512]{2,1,0:T(8,128)S(1)}, u32[]{:S(2)}, u32[]{:S(2)}) %all-to-all-start.2) | async-done | bytes 786464 | tf_op jit(solution)/shard_map/all_to_all | solution.py:155
  362.4 18.8 %all-reduce = (f32[128]{0:T(128)S(1)}, f32[128]{0:T(128)S(1)}, f32[128,8]{0,1:T(8,128)S(1)}) all-reduce(f32[128]{0:T(128)S(1)} %get-tuple-element.31, f32[128]{0:T(128)S(1)} %fusion.49, f32[128,8]{0,1:T(8,128)S(1)} %fusion.54), channel_id=1, replica_groups=mesh['section'=2,'expert'=8,'hid'=8] {'hid'}, use_global_device_ids=true, to_apply=%region_13.14 | all-reduce | flops 1280 | bytes 10240 | tf_op jit(solution)/shard_map/psum | solution.py:171
  381.5 12.0 %all_to_all.74 = bf16[8,48,512]{2,1,0:T(8,128)(2,1)} all-to-all(bf16[8,48,512]{2,1,0:T(8,128)(2,1)S(1)} %bitcast.151), channel_id=1, replica_groups=mesh['section'=2,'expert'=8,'hid'=8] {'expert'}, dimensions={0} | all-to-all | bytes 786432 | tf_op jit(solution)/shard_map/all_to_all | solution.py:124
  393.6 67.0 %all-gather.8.cloned.1.call-done = bf16[384,4096]{1,0:T(8,128)(2,1)} async-done(((bf16[384,512]{1,0:T(8,128)(2,1)}), bf16[384,4096]{1,0:T(8,128)(2,1)}) %all-gather.8.cloned.1.call-update) | async-done | bytes 3145744 | tf_op jit(solution)/shard_map/all_gather | solution.py:131
  460.6 8.0 %fusion = f32[384,896]{1,0:T(8,128)S(1)} fusion(bf16[384,4096]{1,0:T(8,128)(2,1)} %all-gather.8.cloned.1.call-done, bf16[1,1,4096,896]{3,2,1,0:T(8,128)(2,1)} %param.17), kind=kOutput, calls=%fused_computation.6 | convolution fusion | flops 2818572288 | bytes 11862016 | tf_op jit(solution)/shard_map/dot_general | solution.py:69
  468.6 15.4 %fusion.12 = f32[384,4096]{1,0:T(8,128)} fusion(bf16[1,1,896,4096]{3,2,1,0:T(8,128)(2,1)} %param.19, bf16[384,4096]{1,0:T(8,128)(2,1)} %all-gather.8.cloned.1.call-done, bf16[1,1,4096,896]{3,2,1,0:T(8,128)(2,1)} %param.18, f32[384,896]{1,0:T(8,128)S(1)} %fusion), kind=kOutput, calls=%fused_computation.18 | convolution fusion | flops 5639208960 | bytes 25493504 | tf_op jit(solution)/shard_map/dot_general | solution.py:149
  484.4 130.6 %reduce-scatter.5.cloned.1.call-done = f32[384,512]{1,0:T(8,128)} async-done(((f32[384,4096]{1,0:T(8,128)}), f32[384,512]{1,0:T(8,128)}) %reduce-scatter.5.cloned.1.call-update) | async-done | bytes 786448 | tf_op jit(solution)/shard_map/reduce_scatter | solution.py:152
  615.0 4.4 all-to-all-start.5
  619.7 12.9 %all-to-all-done.5 = f32[8,48,512]{2,1,0:T(8,128)S(1)} async-done(((f32[8,48,512]{2,1,0:T(8,128)}), f32[8,48,512]{2,1,0:T(8,128)S(1)}, u32[]{:S(2)}, u32[]{:S(2)}) %all-to-all-start.5) | async-done | bytes 786464 | tf_op jit(solution)/shard_map/all_to_all | solution.py:157
  (90 shorter events, 25.1 us)
Async XLA Ops:
  7.2 206.5 %copy-start = (f32[1,512,8]{1,2,0:T(8,128)S(1)}, f32[1,512,8]{1,2,0:T(8,128)}, u32[]{:S(2)}) copy-start(f32[1,512,8]{1,2,0:T(8,128)} %param.16) | copy-start | bytes 49156
  7.2 39.4 %copy-start.3 = (bf16[1,128,512]{2,1,0:T(8,128)(2,1)S(1)}, bf16[1,128,512]{2,1,0:T(8,128)(2,1)}, u32[]{:S(2)}) copy-start(bf16[1,128,512]{2,1,0:T(8,128)(2,1)} %param.11) | copy-start | bytes 393220
  7.2 106.3 %all-gather.6.cloned.1.call-start = ((), (), s32[]{:S(2)}) async-start(), calls=%async_computation.9 | async-start | bytes 3538944 | tf_op jit(solution)/shard_map/all_gather | solution.py:129
  46.5 139.8 %all-gather.4.cloned.1.call-start = ((), (), s32[]{:S(2)}) async-start(), calls=%async_computation.8 | async-start | bytes 3538944 | tf_op jit(solution)/shard_map/all_gather | solution.py:130
  58.9 283.9 %reduce-scatter.3.cloned.1.call-start = ((), (), s32[]{:S(2)}) async-start(), calls=%async_computation.10 | async-start | bytes 7077888 | tf_op jit(solution)/shard_map/reduce_scatter | solution.py:151
  113.5 9.0 %copy-start.6 = (bf16[384,4096]{1,0:T(8,128)(2,1)S(1)}, bf16[384,4096]{1,0:T(8,128)(2,1)}, u32[]{:S(2)}) copy-start(bf16[384,4096]{1,0:T(8,128)(2,1)} %all-gather.6.cloned.1.call-done) | copy-start | bytes 9437188
  211.0 0.7 copy-start.5
  211.0 2.7 copy-start.1
  211.0 2.7 copy-start.4
  211.6 135.6 %copy-start.2 = (bf16[1,128,512]{2,1,0:T(8,128)(2,1)S(1)}, bf16[1,128,512]{2,1,0:T(8,128)(2,1)}, u32[]{:S(2)}) copy-start(bf16[1,128,512]{2,1,0:T(8,128)(2,1)} %param.12) | copy-start | bytes 393220
  240.3 9.7 %all-to-all-start.3 = ((f32[8,48,1]{1,2,0:T(1,128)}), f32[8,48,1]{1,2,0:T(1,128)S(1)}, u32[]{:S(2)}, u32[]{:S(2)}) async-start(f32[8,48,1]{1,2,0:T(1,128)} %bitcast.18), calls=%async_computation.4 | async-start | bytes 8192 | tf_op jit(solution)/shard_map/all_to_all | solution.py:156
  342.7 17.6 %all-to-all-start.2 = ((f32[8,48,512]{2,1,0:T(8,128)}), f32[8,48,512]{2,1,0:T(8,128)S(1)}, u32[]{:S(2)}, u32[]{:S(2)}) async-start(f32[8,48,512]{2,1,0:T(8,128)} %bitcast.153), calls=%async_computation.3 | async-start | bytes 1572864 | tf_op jit(solution)/shard_map/all_to_all | solution.py:155
  347.2 113.5 %all-gather.8.cloned.1.call-start = ((), (), s32[]{:S(2)}) async-start(), calls=%async_computation.11 | async-start | bytes 3538944 | tf_op jit(solution)/shard_map/all_gather | solution.py:131
  393.5 221.5 %reduce-scatter.5.cloned.1.call-start = ((), (), s32[]{:S(2)}) async-start(), calls=%async_computation.12 | async-start | bytes 7077888 | tf_op jit(solution)/shard_map/reduce_scatter | solution.py:152
  615.0 17.6 %all-to-all-start.5 = ((f32[8,48,512]{2,1,0:T(8,128)}), f32[8,48,512]{2,1,0:T(8,128)S(1)}, u32[]{:S(2)}, u32[]{:S(2)}) async-start(f32[8,48,512]{2,1,0:T(8,128)} %bitcast.154), calls=%async_computation.7 | async-start | bytes 1572864 | tf_op jit(solution)/shard_map/all_to_all | solution.py:157
  634.3 6.6 %collective-permute-start = (bf16[128,512]{1,0:T(8,128)(2,1)S(1)}, bf16[128,512]{1,0:T(8,128)(2,1)S(1)}, u32[]{:S(2)}, u32[]{:S(2)}) collective-permute-start(bf16[128,512]{1,0:T(8,128)(2,1)S(1)} %get-tuple-element.19), channel_id=1, source_target_pairs={{0,64},{64,0},{1,65},{65,1},{2,66},{66,2},{3,67},{67,3},{4,68},{68... | collective-permute-start | bytes 393224 | tf_op jit(solution)/shard_map/ppermute | solution.py:18
Sparse Core Ops, SparseCore 0:
  46.6 66.7 all-gather.5
  115.1 71.1 all-gather.3
  211.1 131.5 reduce-scatter.2
  393.7 66.9 all-gather.7
  484.2 130.8 reduce-scatter.4
where the time goes:
time: 649 us; the launch traced here: 648 us
  waiting for transfers between devices  433 us (67%)
  blocking collectives  103 us (16%)
  matrix products  65.6 us (10%)
  starting transfers between devices  16.3 us (3%)
  between operations  14.1 us (2%)
  local copies, waits for them, and re-layouts  10.5 us (2%)
    reduce_scatter x1, waiting for transfers between devices, per_device(): lax.psum_scatter(out_part, 'hid', scatter_dimension=1, tiled=True)  131 us
    reduce_scatter x1, waiting for transfers between devices, per_device(): lax.psum_scatter(back_part, 'hid', scatter_dimension=1, tiled=True)  92.7 us
    all_gather x1, waiting for transfers between devices, per_device(): lax.all_gather(moved[2], 'hid', axis=1, tiled=True)  67 us
    all_gather x1, waiting for transfers between devices, per_device(): lax.all_gather(moved[1], 'hid', axis=1, tiled=True)  58.1 us
    all_gather x1, waiting for transfers between devices, per_device(): lax.all_gather(moved[0], 'hid', axis=1, tiled=True)  54.5 us
    psum x2, blocking collectives, per_device(): lax.psum((squares_saved, partial_saved, squares_next, partial_next), 'hid')  46.2 us
    psum x1, blocking collectives, per_device(): inner = lax.psum(jnp.sum(scaled_grad * values_saved, axis=1), 'hid')  18.8 us
    dot_general x1, matrix products, per_device(): jnp.dot(hidden_next, down_matrix, preferred_element_type=jnp.float32)  15.4 us
  transfers between devices with their start and end apart: 9, of which 9 were waited for; matrix products, arithmetic and copies ran while one was open for 4% of the time, Pallas kernels for 0%

commit v1 on v0

--- a/solution.py
+++ b/solution.py
@@ -168,7 +168,9 @@
         grad_logit[:, None] * diff_saved, table.T, precision=HIGHEST
     )
     scaled_grad = grad_normed * gain[None, :]
-    inner = lax.psum(jnp.sum(scaled_grad * values_saved, axis=1), "hid")
+    inner = jnp.sum(
+        jax.lax.all_gather(jnp.sum(scaled_grad * values_saved, axis=1), axis_name="hid"), axis=0
+    )
     cube = scale_saved * scale_saved * scale_saved
     grad_input = (
         cot_rows.astype(jnp.float32)

time: 649 us -> 615 us (0.948)
  waiting for transfers between devices: 433 us -> 390 us
  blocking collectives: 103 us -> 110 us
    psum x1 -> x0, blocking collectives: 18.8 us -> none  [per_device(): inner = lax.psum(jnp.sum(scaled_grad * values_saved, axis=1), 'hid')]
    all_gather x0 -> x1, blocking collectives: none -> 17.6 us  [per_device(): jax.lax.all_gather(jnp.sum(scaled_grad * values_saved, axis=1), axis_name...]
    all_gather x1, waiting for transfers between devices: 67 us -> 50.3 us  [per_device(): lax.all_gather(moved[2], 'hid', axis=1, tiled=True)]
    reduce_scatter x1, waiting for transfers between devices: 131 us -> 115 us  [per_device(): lax.psum_scatter(out_part, 'hid', scatter_dimension=1, tiled=True)]
    all_to_all x1, waiting for transfers between devices: 12.9 us -> 0.01 us  [per_device(): lax.all_to_all(out_sum, 'expert', split_axis=0, concat_axis=0, tiled=True)]
    psum x2, blocking collectives: 46.2 us -> 52.8 us  [per_device(): lax.psum((squares_saved, partial_saved, squares_next, partial_next), 'hid')]
  transfers between devices with their start and end apart: 9 -> 9, of which waited for: 9 -> 8; matrix products, arithmetic and copies ran while one was open for 4% -> 11% of each run, Pallas kernels for 0% -> 0%
where the time goes in v1:
time: 615 us; the launch traced here: 614 us
  waiting for transfers between devices  390 us (63%)
  blocking collectives  110 us (18%)
  matrix products  67 us (11%)
  starting transfers between devices  17.1 us (3%)
  between operations  14.1 us (2%)
  local copies, waits for them, and re-layouts  9.88 us (2%)
    reduce_scatter x1, waiting for transfers between devices, per_device(): lax.psum_scatter(out_part, 'hid', scatter_dimension=1, tiled=True)  115 us
    reduce_scatter x1, waiting for transfers between devices, per_device(): lax.psum_scatter(back_part, 'hid', scatter_dimension=1, tiled=True)  98.6 us
    all_gather x1, waiting for transfers between devices, per_device(): lax.all_gather(moved[1], 'hid', axis=1, tiled=True)  57.2 us
    psum x2, blocking collectives, per_device(): lax.psum((squares_saved, partial_saved, squares_next, partial_next), 'hid')  52.8 us
    all_gather x1, waiting for transfers between devices, per_device(): lax.all_gather(moved[0], 'hid', axis=1, tiled=True)  52.2 us
    all_gather x1, waiting for transfers between devices, per_device(): lax.all_gather(moved[2], 'hid', axis=1, tiled=True)  50.3 us
    all_gather x1, blocking collectives, per_device(): jax.lax.all_gather(jnp.sum(scaled_grad * values_saved, axis=1), axis_name...  17.6 us
    dot_general x1, matrix products, per_device(): jnp.dot(hidden_next, down_matrix, preferred_element_type=jnp.float32)  16 us
  transfers between devices with their start and end apart: 9, of which 8 were waited for; matrix products, arithmetic and copies ran while one was open for 11% of the time, Pallas kernels for 0%

profile of v1, /device:TPU:0, one launch (start us, length us, event | category | flops | bytes accessed | tf_op | source)
XLA Modules:
  0.0 613.9 jit_solution(8567528217669775395)
XLA Ops:
  11.3 19.8 %psum.35 = f32[128]{0:T(128)S(1)} all-reduce(f32[128]{0:T(128)S(1)} %fusion.39), channel_id=1, replica_groups=mesh['section'=2,'expert'=8,'hid'=8] {'hid'}, use_global_device_ids=true, to_apply=%region_1.0 | all-reduce | flops 128 | bytes 1024 | tf_op jit(solution)/shard_map/psum | solution.py:98
  32.4 14.2 %all_to_all.72 = bf16[8,48,512]{2,1,0:T(8,128)(2,1)} all-to-all(bf16[8,48,512]{2,1,0:T(8,128)(2,1)S(1)} %bitcast.153), channel_id=1, replica_groups=mesh['section'=2,'expert'=8,'hid'=8] {'expert'}, dimensions={0} | all-to-all | bytes 786432 | tf_op jit(solution)/shard_map/all_to_all | solution.py:122
  46.9 12.0 %all_to_all.73 = bf16[8,48,512]{2,1,0:T(8,128)(2,1)} all-to-all(bf16[8,48,512]{2,1,0:T(8,128)(2,1)S(1)} %bitcast.151), channel_id=1, replica_groups=mesh['section'=2,'expert'=8,'hid'=8] {'expert'}, dimensions={0} | all-to-all | bytes 786432 | tf_op jit(solution)/shard_map/all_to_all | solution.py:123
  61.4 52.2 %all-gather.8.cloned.1.call-done = bf16[384,4096]{1,0:T(8,128)(2,1)} async-done(((bf16[384,512]{1,0:T(8,128)(2,1)}), bf16[384,4096]{1,0:T(8,128)(2,1)}) %all-gather.8.cloned.1.call-update) | async-done | bytes 3145744 | tf_op jit(solution)/shard_map/all_gather | solution.py:129
  113.5 8.9 %fusion.4 = f32[384,896]{1,0:T(8,128)S(1)} fusion(bf16[384,4096]{1,0:T(8,128)(2,1)} %all-gather.8.cloned.1.call-done, bf16[1,1,4096,896]{3,2,1,0:T(8,128)(2,1)} %param.17), kind=kOutput, calls=%fused_computation.10 | convolution fusion | flops 2818572288 | bytes 11862016 | tf_op jit(solution)/shard_map/dot_general | solution.py:64
  122.5 6.7 %fusion.10 = f32[384,896]{1,0:T(8,128)} fusion(bf16[384,4096]{1,0:T(8,128)(2,1)S(1)} %copy-done.6, bf16[1,1,4096,896]{3,2,1,0:T(8,128)(2,1)} %param.18), kind=kOutput, calls=%fused_computation.16 | convolution fusion | flops 2818572288 | bytes 11862016 | tf_op jit(solution)/shard_map/dot_general | solution.py:65
  129.2 57.2 %all-gather.6.cloned.1.call-done = bf16[384,4096]{1,0:T(8,128)(2,1)} async-done(((bf16[384,512]{1,0:T(8,128)(2,1)}), bf16[384,4096]{1,0:T(8,128)(2,1)}) %all-gather.6.cloned.1.call-update) | async-done | bytes 3145744 | tf_op jit(solution)/shard_map/all_gather | solution.py:130
  186.3 7.9 %multiply_reduce_fusion = (f32[384]{0:T(512)S(1)}, f32[384,896]{1,0:T(8,128)S(1)}) fusion(f32[384,896]{1,0:T(8,128)} %fusion.10, f32[384,896]{1,0:T(8,128)S(1)} %fusion.4, bf16[384,4096]{1,0:T(8,128)(2,1)} %all-gather.6.cloned.1.call-done, bf16[1,1,896,4096]{3,2,1,0:T(8,128)(2,1)} %param.19), kind=kOutput, calls=%fused_computation.24 | convolution fusion | flops 2821668352 | bytes 14616064 | tf_op jit(solution)/shard_map/dot_general | solution.py:66
  194.3 33.0 %all-reduce = (f32[128,8]{0,1:T(8,128)S(1)}, f32[8,48,1]{1,0,2:T(8,128)}, f32[128]{0:T(128)S(1)}, f32[128,8]{0,1:T(8,128)S(1)}) all-reduce(f32[128,8]{0,1:T(8,128)S(1)} %fusion.47, f32[8,48,1]{1,0,2:T(8,128)S(1)} %all_to_all.57, f32[128]{0:T(128)S(1)} %fusion.49, ...), channel_id=1, replica_groups=mesh['section'=2,'expert'=8,'hid'=8] {'hid'}, use_global_device_ids=true, to_apply=%region_2.0 | all-reduce | flops 2560 | bytes 20480 | tf_op jit(solution)/shard_map/psum | solution.py:98
  227.6 13.5 %all_to_all.74 = bf16[8,48,512]{2,1,0:T(8,128)(2,1)} all-to-all(bf16[8,48,512]{2,1,0:T(8,128)(2,1)S(1)} %bitcast.152), channel_id=1, replica_groups=mesh['section'=2,'expert'=8,'hid'=8] {'expert'}, dimensions={0} | all-to-all | bytes 786432 | tf_op jit(solution)/shard_map/all_to_all | solution.py:124
  241.4 6.4 %fusion.2 = f32[384,4096]{1,0:T(8,128)S(1)} fusion(bf16[1,1,4096,896]{3,2,1,0:T(8,128)(2,1)} %param.17, f32[384,896]{1,0:T(8,128)S(1)} %fusion.4, f32[384,896]{1,0:T(8,128)S(1)} %get-tuple-element.29, f32[384,896]{1,0:T(8,128)} %fusion.10), kind=kOutput, calls=%fused_computation.8 | convolution fusion | flops 2822012928 | bytes 17760256 | tf_op jit(solution)/shard_map/dot_general | solution.py:144
  247.8 10.1 %fusion.16 = f32[384,4096]{1,0:T(8,128)} fusion(f32[384,4096]{1,0:T(8,128)S(1)} %fusion.2, bf16[1,1,4096,896]{3,2,1,0:T(8,128)(2,1)} %param.18, f32[384,896]{1,0:T(8,128)S(1)} %get-tuple-element.29, f32[384,896]{1,0:T(8,128)S(1)} %fusion.4), kind=kOutput, calls=%fused_computation.22 | convolution fusion | flops 2822209536 | bytes 22675456 | tf_op jit(solution)/shard_map/dot_general | solution.py:146
  258.0 50.3 %all-gather.10.cloned.1.call-done = bf16[384,4096]{1,0:T(8,128)(2,1)} async-done(((bf16[384,512]{1,0:T(8,128)(2,1)}), bf16[384,4096]{1,0:T(8,128)(2,1)}) %all-gather.10.cloned.1.call-update) | async-done | bytes 3145744 | tf_op jit(solution)/shard_map/all_gather | solution.py:131
  308.2 8.0 %fusion = f32[384,896]{1,0:T(8,128)S(1)} fusion(bf16[384,4096]{1,0:T(8,128)(2,1)} %all-gather.10.cloned.1.call-done, bf16[1,1,4096,896]{3,2,1,0:T(8,128)(2,1)} %param.17), kind=kOutput, calls=%fused_computation.6 | convolution fusion | flops 2818572288 | bytes 11862016 | tf_op jit(solution)/shard_map/dot_general | solution.py:69
  316.2 16.0 %fusion.12 = f32[384,4096]{1,0:T(8,128)} fusion(bf16[1,1,896,4096]{3,2,1,0:T(8,128)(2,1)} %param.19, bf16[384,4096]{1,0:T(8,128)(2,1)} %all-gather.10.cloned.1.call-done, bf16[1,1,4096,896]{3,2,1,0:T(8,128)(2,1)} %param.18, f32[384,896]{1,0:T(8,128)S(1)} %fusion), kind=kOutput, calls=%fused_computation.18 | convolution fusion | flops 5639208960 | bytes 25493504 | tf_op jit(solution)/shard_map/dot_general | solution.py:149
  332.8 4.8 all-to-all-start.3
  337.8 5.0 all-to-all-done.3
  342.8 98.6 %reduce-scatter.3.cloned.1.call-done = f32[384,512]{1,0:T(8,128)} async-done(((f32[384,4096]{1,0:T(8,128)}), f32[384,512]{1,0:T(8,128)}) %reduce-scatter.3.cloned.1.call-update) | async-done | bytes 786448 | tf_op jit(solution)/shard_map/reduce_scatter | solution.py:151
  441.4 4.4 all-to-all-start.2
  450.0 8.9 %all-to-all-done.2 = f32[8,48,512]{2,1,0:T(8,128)S(1)} async-done(((f32[8,48,512]{2,1,0:T(8,128)}), f32[8,48,512]{2,1,0:T(8,128)S(1)}, u32[]{:S(2)}, u32[]{:S(2)}) %all-to-all-start.2) | async-done | bytes 786464 | tf_op jit(solution)/shard_map/all_to_all | solution.py:155
  458.9 115.4 %reduce-scatter.5.cloned.1.call-done = f32[384,512]{1,0:T(8,128)} async-done(((f32[384,4096]{1,0:T(8,128)}), f32[384,512]{1,0:T(8,128)}) %reduce-scatter.5.cloned.1.call-update) | async-done | bytes 786448 | tf_op jit(solution)/shard_map/reduce_scatter | solution.py:152
  574.3 4.4 all-to-all-start.5
  580.8 17.6 %all-gather.1 = f32[8,1,128]{2,1,0:T(1,128)S(1)} all-gather(f32[1,1,128]{2,1,0:T(1,128)S(1)} %bitcast.162), channel_id=2, replica_groups=mesh['section'=2,'expert'=8,'hid'=8] {'hid'}, dimensions={0}, use_global_device_ids=true | all-gather | bytes 4608 | tf_op jit(solution)/shard_map/all_gather | solution.py:172
  600.2 3.1 collective-permute-start
  (90 shorter events, 21.5 us)
Async XLA Ops:
  7.2 53.6 %copy-start = (f32[1,512,8]{1,2,0:T(8,128)S(1)}, f32[1,512,8]{1,2,0:T(8,128)}, u32[]{:S(2)}) copy-start(f32[1,512,8]{1,2,0:T(8,128)} %param.16) | copy-start | bytes 49156
  7.2 39.4 %copy-start.3 = (bf16[1,128,512]{2,1,0:T(8,128)(2,1)S(1)}, bf16[1,128,512]{2,1,0:T(8,128)(2,1)}, u32[]{:S(2)}) copy-start(bf16[1,128,512]{2,1,0:T(8,128)(2,1)} %param.11) | copy-start | bytes 393220
  7.2 106.3 %all-gather.8.cloned.1.call-start = ((), (), s32[]{:S(2)}) async-start(), calls=%async_computation.9 | async-start | bytes 3538944 | tf_op jit(solution)/shard_map/all_gather | solution.py:129
  32.3 26.6 %copy-start.5 = (s32[1,128,2]{1,2,0:T(2,128)S(1)}, s32[1,128,2]{1,2,0:T(2,128)}, u32[]{:S(2)}) copy-start(s32[1,128,2]{1,2,0:T(2,128)} %param.14) | copy-start | bytes 3076
  46.5 14.1 %copy-start.2 = (bf16[1,128,512]{2,1,0:T(8,128)(2,1)S(1)}, bf16[1,128,512]{2,1,0:T(8,128)(2,1)}, u32[]{:S(2)}) copy-start(bf16[1,128,512]{2,1,0:T(8,128)(2,1)} %param.12) | copy-start | bytes 393220
  46.5 14.2 %copy-start.1 = (bf16[1,128,512]{2,1,0:T(8,128)(2,1)S(1)}, bf16[1,128,512]{2,1,0:T(8,128)(2,1)}, u32[]{:S(2)}) copy-start(bf16[1,128,512]{2,1,0:T(8,128)(2,1)} %param.10) | copy-start | bytes 393220
  46.5 14.2 %copy-start.4 = (f32[1,512]{1,0:T(1,128)S(1)}, f32[1,512]{1,0:T(1,128)}, u32[]{:S(2)}) copy-start(f32[1,512]{1,0:T(1,128)} %param.15) | copy-start | bytes 6148
  46.5 139.8 %all-gather.6.cloned.1.call-start = ((), (), s32[]{:S(2)}) async-start(), calls=%async_computation.8 | async-start | bytes 3538944 | tf_op jit(solution)/shard_map/all_gather | solution.py:130
  58.9 249.3 %all-gather.10.cloned.1.call-start = ((), (), s32[]{:S(2)}) async-start(), calls=%async_computation.11 | async-start | bytes 3538944 | tf_op jit(solution)/shard_map/all_gather | solution.py:131
  113.5 8.9 %copy-start.6 = (bf16[384,4096]{1,0:T(8,128)(2,1)S(1)}, bf16[384,4096]{1,0:T(8,128)(2,1)}, u32[]{:S(2)}) copy-start(bf16[384,4096]{1,0:T(8,128)(2,1)} %all-gather.8.cloned.1.call-done) | copy-start | bytes 9437188
  241.2 200.2 %reduce-scatter.3.cloned.1.call-start = ((), (), s32[]{:S(2)}) async-start(), calls=%async_computation.10 | async-start | bytes 7077888 | tf_op jit(solution)/shard_map/reduce_scatter | solution.py:151
  257.9 316.3 %reduce-scatter.5.cloned.1.call-start = ((), (), s32[]{:S(2)}) async-start(), calls=%async_computation.12 | async-start | bytes 7077888 | tf_op jit(solution)/shard_map/reduce_scatter | solution.py:152
  332.8 10.0 %all-to-all-start.3 = ((f32[8,48,1]{1,2,0:T(1,128)}), f32[8,48,1]{1,2,0:T(1,128)S(1)}, u32[]{:S(2)}, u32[]{:S(2)}) async-start(f32[8,48,1]{1,2,0:T(1,128)} %bitcast.18), calls=%async_computation.4 | async-start | bytes 8192 | tf_op jit(solution)/shard_map/all_to_all | solution.py:156
  441.4 17.6 %all-to-all-start.2 = ((f32[8,48,512]{2,1,0:T(8,128)}), f32[8,48,512]{2,1,0:T(8,128)S(1)}, u32[]{:S(2)}, u32[]{:S(2)}) async-start(f32[8,48,512]{2,1,0:T(8,128)} %bitcast.155), calls=%async_computation.3 | async-start | bytes 1572864 | tf_op jit(solution)/shard_map/all_to_all | solution.py:155
  574.3 24.2 %all-to-all-start.5 = ((f32[8,48,512]{2,1,0:T(8,128)}), f32[8,48,512]{2,1,0:T(8,128)S(1)}, u32[]{:S(2)}, u32[]{:S(2)}) async-start(f32[8,48,512]{2,1,0:T(8,128)} %bitcast.154), calls=%async_computation.7 | async-start | bytes 1572864 | tf_op jit(solution)/shard_map/all_to_all | solution.py:157
  600.2 6.6 %collective-permute-start = (bf16[128,512]{1,0:T(8,128)(2,1)S(1)}, bf16[128,512]{1,0:T(8,128)(2,1)S(1)}, u32[]{:S(2)}, u32[]{:S(2)}) collective-permute-start(bf16[128,512]{1,0:T(8,128)(2,1)S(1)} %get-tuple-element.18), channel_id=1, source_target_pairs={{0,64},{64,0},{1,65},{65,1},{2,66},{66,2},{3,67},{67,3},{4,68},{68... | collective-permute-start | bytes 393224 | tf_op jit(solution)/shard_map/ppermute | solution.py:18
Sparse Core Ops, SparseCore 0:
  46.7 66.7 all-gather.7
  115.2 71.1 all-gather.5
  241.3 66.9 all-gather.9
  310.5 130.8 reduce-scatter.2
  443.6 130.6 reduce-scatter.4
